TPU v7x, 128 devices: a whole 4x4x4 slice. The times are simulated.
128 devices in a mesh: row: 16 (over z, y), col: 8 (over x, core).
Axes of the slice: x: 4, y: 4, z: 4, core: 2. Of those that a mesh axis runs over, the one named last changes fastest.
Arguments:
- covariance: float32 [4, 16, 256, 8, 8, 256], P(None, 'row', None, None, 'col'), as said below
- check_weights: float32 [4, 16, 256], P(None, 'row'), may hold values from 0.05 to 0.5
Outputs:
- trailing: float32 [4, 16, 256, 8, 8, 256], P(None, 'row', None, None, 'col')
- panels: float32 [4, 16, 256, 512], P(None, 'row')
- checksum: float32 [8, 8, 256], P(None, 'col')
Inputs may be any that keep to these rules, and one draw needn't show every extreme that they name: covariance is symmetric with smallest eigenvalue at least 0.5: an exponential kernel of jittered grid sites plus a nugget plus a small symmetric rough part.
All inputs are finite; a program needn't handle non-finite values.
Results may differ from a plain program's by a relative error of at most 0.0003.
Values sent between devices are 32-bit elements; how exact they have to be, the bound alone decides.
No kernel may reach another device: no remote copies, remote signals or barrier semaphores. Data moves between devices by JAX's collectives and lax.ppermute only.
A program may use at most 128 MiB of HBM per device.

v0:
```python
import jax
import jax.numpy as jnp
from jax import lax
from jax.sharding import PartitionSpec as P

HIGHEST = lax.Precision.HIGHEST


def from_root(value, axis, source):
    kept = jnp.where(lax.axis_index(axis) == source, value, 0).astype(value.dtype)
    return lax.psum(kept, axis)


def shards(covariance, check_weights):
    rows_size = lax.axis_size("row")
    cols_size = lax.axis_size("col")
    row_tiles = covariance.shape[0]
    width = covariance.shape[2]
    col_tiles = covariance.shape[3]
    matrix = covariance.reshape(row_tiles, width, col_tiles, width)
    row_index = lax.axis_index("row")
    col_index = lax.axis_index("col")
    global_rows = jnp.arange(row_tiles, dtype=jnp.int32) * rows_size + row_index
    global_cols = jnp.arange(col_tiles, dtype=jnp.int32) * cols_size + col_index
    panel_list = []
    for step in range(2):
        corner = matrix[step // rows_size, :, step // cols_size, :]
        corner = from_root(corner, "row", step % rows_size)
        corner = jnp.where(col_index == step % cols_size, corner, jnp.eye(width, dtype=jnp.float32))
        factor = jnp.linalg.cholesky(corner)
        column = matrix[:, :, step // cols_size, :].reshape(row_tiles * width, width)
        solved = jax.scipy.linalg.solve_triangular(factor, column.T, lower=True).T
        solved = solved.reshape(row_tiles, width, width)
        solved = jnp.where((global_rows >= step)[:, None, None], solved, 0.0)
        solved = from_root(solved, "col", step % cols_size)
        whole = lax.all_gather(solved, "row", axis=0, tiled=True)
        picked = global_cols % rows_size * row_tiles + global_cols // rows_size
        across = jnp.take(whole, picked, axis=0)
        matrix = matrix - jnp.einsum("iak,jbk->iajb", solved, across, precision=HIGHEST)
        panel_list.append(solved)
    keep = (global_rows >= 2)[:, None, None, None] & (global_cols >= 2)[None, None, :, None]
    trailing = jnp.where(keep, matrix, 0.0)
    weights = check_weights.reshape(row_tiles, width)
    partial_sums = jnp.einsum("ia,iajb->jb", weights, trailing, precision=HIGHEST)
    checksum = lax.psum(partial_sums, "row")
    panels = jnp.concatenate(panel_list, axis=2)
    return (
        trailing.reshape(row_tiles, 1, width, col_tiles, 1, width),
        panels.reshape(row_tiles, 1, width, 2 * width),
        checksum.reshape(col_tiles, 1, width),
    )


def solution(mesh):
    in_specs = (P(None, "row", None, None, "col", None), P(None, "row", None))
    out_specs = (
        P(None, "row", None, None, "col", None),
        P(None, "row", None, None),
        P(None, "col", None),
    )
    return jax.shard_map(shards, mesh=mesh, in_specs=in_specs, out_specs=out_specs, check_vma=False)
```

profile of v0, /device:TPU:0, one launch (start us, length us, event | category | flops | bytes accessed | tf_op | source)
XLA Modules:
  0.0 790.6 jit_solution(16580449472333877571)
XLA Ops:
  7.2 20.6 %copy.25 = f32[4,1,256,8,1,256]{2,5,3,0,4,1:T(8,128)} copy(f32[4,1,256,8,1,256]{5,4,3,2,1,0:T(1,128)} %param.7) | data formatting | bytes 16777216 | tf_op args[0]
  27.8 1.7 fusion.15
  29.5 1.3 slice.67
  31.5 85.0 %all-reduce.6.cloned.1.call-done = f32[256,256]{0,1:T(8,128)} async-done(((f32[256,256]{0,1:T(8,128)}), f32[256,256]{0,1:T(8,128)}) %all-reduce.6.cloned.1.call-update) | async-done | bytes 262160 | tf_op jit(solution)/shard_map/psum | solution.py:11
  116.6 1.0 convert_select_fusion.1
  117.7 1.0 fusion.17
  118.7 11.7 %cholesky.130 = f32[128,128]{1,0:T(8,128)S(1)} custom-call(f32[128,128]{1,0:T(8,128)S(1)} %cholesky.194), custom_call_target="Cholesky" | custom-call | tf_op jit(solution)/shard_map/jit(cholesky)/cholesky | solution.py:30
  130.4 9.8 %custom-call.13 = f32[1,128,128]{1,2,0:T(8,128)S(1)} custom-call(f32[1,128,128]{2,1,0:T(8,128)S(1)} %get-tuple-element.58), custom_call_target="InvertDiagBlocksLowerTriangular" | custom-call | tf_op jit(solution)/shard_map/jit(cholesky)/cholesky | solution.py:30
  140.8 11.7 %cholesky.147 = f32[128,128]{1,0:T(8,128)S(1)} custom-call(f32[128,128]{1,0:T(8,128)S(1)} %convolution_subtract_fusion.4), custom_call_target="Cholesky" | custom-call | tf_op jit(solution)/shard_map/jit(cholesky)/cholesky | solution.py:30
  152.5 0.7 compare_reduce_fusion.2
  154.7 4.6 while.4
  155.2 0.6 fusion.48
  155.8 1.4 bitcast_dynamic-update-slice_fusion.4
  157.3 0.6 fusion.48
  157.9 1.4 bitcast_dynamic-update-slice_fusion.4
  159.3 19.7 %custom-call.14 = f32[2,128,128]{1,2,0:T(8,128)S(1)} custom-call(f32[2,128,128]{2,1,0:T(8,128)S(1)} %get-tuple-element.20), custom_call_target="InvertDiagBlocksLowerTriangular" | custom-call | tf_op jit(solution)/shard_map/jit(_solve_triangular)/triangular_solve | solution.py:32
  179.0 0.6 fusion.12
  180.2 0.6 fusion.23
  181.3 1.2 select_select_fusion.1
  182.5 59.7 %all-reduce.8.cloned.1.call-done = f32[4,256,256]{2,1,0:T(8,128)} async-done(((f32[4,256,256]{2,1,0:T(8,128)}), f32[4,256,256]{2,1,0:T(8,128)}) %all-reduce.8.cloned.1.call-update) | async-done | bytes 1048592 | tf_op jit(solution)/shard_map/psum | solution.py:11
  242.4 113.1 %all-gather.3.cloned.1.call-done = f32[64,256,256]{2,1,0:T(8,128)} async-done(((f32[4,256,256]{2,1,0:T(8,128)}), f32[64,256,256]{2,1,0:T(8,128)}) %all-gather.3.cloned.1.call-update) | async-done | bytes 16777232 | tf_op jit(solution)/shard_map/all_gather | solution.py:36
  355.4 7.8 gather_fusion
  363.2 9.6 %convolution_subtract_fusion = f32[4,256,8,256]{1,3,2,0:T(8,128)S(1)} fusion(f32[8,256,256]{2,1,0:T(8,128)} %gather_fusion, f32[4,256,256]{2,1,0:T(8,128)S(1)} %copy-done.3, pred[8]{0:T(512)(128)(4,1)S(1)} %compare_and_fusion, f32[4,1,256,8,1,256]{2,5,3,0,4,1:T(8,128)} %copy.25), kind=kOutput, calls=%fused_computation.7 | convolution fusion | flops 6445072384 | bytes 19922952 | tf_op jit(solution)/shard_map/iak,jbk->iajb/dot_general | solution.py:39
  372.8 3.4 copy-done.2
  376.2 0.7 fusion.14
  377.2 1.0 slice-done
  378.8 82.3 %all-reduce.10.cloned.1.call-done = f32[256,256]{0,1:T(8,128)} async-done(((f32[256,256]{0,1:T(8,128)}), f32[256,256]{0,1:T(8,128)}) %all-reduce.10.cloned.1.call-update) | async-done | bytes 262160 | tf_op jit(solution)/shard_map/psum | solution.py:11
  461.4 11.7 %cholesky.164 = f32[128,128]{1,0:T(8,128)S(1)} custom-call(f32[128,128]{1,0:T(8,128)S(1)} %cholesky.197), custom_call_target="Cholesky" | custom-call | tf_op jit(solution)/shard_map/jit(cholesky)/cholesky | solution.py:30
  473.1 0.6 compare_reduce_fusion.1
  473.8 9.8 %custom-call.15 = f32[1,128,128]{1,2,0:T(8,128)S(1)} custom-call(f32[1,128,128]{2,1,0:T(8,128)S(1)} %get-tuple-element.54), custom_call_target="InvertDiagBlocksLowerTriangular" | custom-call | tf_op jit(solution)/shard_map/jit(cholesky)/cholesky | solution.py:30
  484.1 11.7 %cholesky.181 = f32[128,128]{1,0:T(8,128)S(1)} custom-call(f32[128,128]{1,0:T(8,128)S(1)} %convolution_subtract_fusion.3), custom_call_target="Cholesky" | custom-call | tf_op jit(solution)/shard_map/jit(cholesky)/cholesky | solution.py:30
  495.9 0.7 compare_reduce_fusion
  498.0 4.3 while.5
  498.2 0.6 fusion.49
  498.8 1.4 bitcast_dynamic-update-slice_fusion.5
  500.9 1.4 bitcast_dynamic-update-slice_fusion.5
  502.3 19.7 %custom-call.16 = f32[2,128,128]{1,2,0:T(8,128)S(1)} custom-call(f32[2,128,128]{2,1,0:T(8,128)S(1)} %get-tuple-element.21), custom_call_target="InvertDiagBlocksLowerTriangular" | custom-call | tf_op jit(solution)/shard_map/jit(_solve_triangular)/triangular_solve | solution.py:32
  522.0 0.6 fusion.10
  523.2 0.6 fusion.19
  524.3 1.2 select_select_fusion
  525.5 61.7 %all-reduce.12.cloned.1.call-done = f32[4,256,256]{2,1,0:T(8,128)} async-done(((f32[4,256,256]{2,1,0:T(8,128)}), f32[4,256,256]{2,1,0:T(8,128)}) %all-reduce.12.cloned.1.call-update) | async-done | bytes 1048592 | tf_op jit(solution)/shard_map/psum | solution.py:11
  587.3 2.8 maximum_bitcast_fusion
  590.1 109.9 %all-gather.5.cloned.1.call-done = f32[64,256,256]{2,1,0:T(8,128)} async-done(((f32[4,256,256]{2,1,0:T(8,128)}), f32[64,256,256]{2,1,0:T(8,128)}) %all-gather.5.cloned.1.call-update) | async-done | bytes 16777232 | tf_op jit(solution)/shard_map/all_gather | solution.py:36
  700.0 6.4 gather_fusion.1
  706.5 9.6 %subtract_select_fusion = f32[4,256,8,256]{1,3,2,0:T(8,128)S(1)} fusion(f32[4,256,8,256]{1,3,2,0:T(8,128)} %copy-done.2, pred[4,8]{1,0:T(4,128)(4,1)S(1)} %broadcast_and_fusion, f32[8,256,256]{2,1,0:T(8,128)S(1)} %gather_fusion.1, f32[4,256,256]{2,1,0:T(8,128)S(1)} %copy-done.4, pred[8]{0:T(512)(128)(4,1)S(1)} %compare_and_fusion), kind=kOutput, calls=%fused_computation.6 | convolution fusion | flops 6447169536 | bytes 19922984 | tf_op jit(solution)/shard_map/iak,jbk->iajb/dot_general | solution.py:39
  716.1 7.2 fusion.28
  723.3 39.5 %psum.39 = f32[8,1,256]{2,1,0:T(1,128)} all-reduce(f32[8,1,256]{2,1,0:T(1,128)S(1)} %reshape.113), channel_id=1, replica_groups=mesh['row'=16,'col'=8] {'row'}, use_global_device_ids=true, to_apply=%region_8.12 | all-reduce | flops 2048 | bytes 16384 | tf_op jit(solution)/shard_map/psum | solution.py:45
  762.9 20.5 %copy.36 = f32[4,1,256,8,1,256]{5,4,3,2,1,0:T(1,128)} copy(f32[4,1,256,8,1,256]{2,5,3,0,4,1:T(8,128)} %bitcast.106) | data formatting | bytes 16777216
  (69 shorter events, 6.3 us)
Async XLA Ops:
  7.2 708.9 %copy-start = (f32[4,1,256]{2,1,0:T(1,128)S(1)}, f32[4,1,256]{2,1,0:T(1,128)}, u32[]{:S(2)}) copy-start(f32[4,1,256]{2,1,0:T(1,128)} %param.8) | copy-start | bytes 12292
  7.2 109.4 %all-reduce.6.cloned.1.call-start = ((), (), s32[]{:S(2)}) async-start(), calls=%async_computation | async-start | bytes 524288 | tf_op jit(solution)/shard_map/psum | solution.py:11
  29.5 212.7 %all-reduce.8.cloned.1.call-start = ((), (), s32[]{:S(2)}) async-start(), calls=%async_computation.1 | async-start | bytes 2097152 | tf_op jit(solution)/shard_map/psum | solution.py:11
  182.5 173.0 %all-gather.3.cloned.1.call-start = ((), (), s32[]{:S(2)}) async-start(), calls=%async_computation.2 | async-start | bytes 17825792 | tf_op jit(solution)/shard_map/all_gather | solution.py:36
  242.2 218.9 %all-reduce.10.cloned.1.call-start = ((), (), s32[]{:S(2)}) async-start(), calls=%async_computation.3 | async-start | bytes 524288 | tf_op jit(solution)/shard_map/psum | solution.py:11
  242.4 120.8 %copy-start.3 = (f32[4,256,256]{2,1,0:T(8,128)S(1)}, f32[4,256,256]{2,1,0:T(8,128)}, u32[]{:S(2)}) copy-start(f32[4,256,256]{2,1,0:T(8,128)} %all-reduce.8.cloned.1.call-done) | copy-start | bytes 3145732
  372.8 3.4 copy-start.2
  376.9 1.2 slice-start
  377.0 210.2 %all-reduce.12.cloned.1.call-start = ((), (), s32[]{:S(2)}) async-start(), calls=%async_computation.4 | async-start | bytes 2097152 | tf_op jit(solution)/shard_map/psum | solution.py:11
  525.5 174.6 %all-gather.5.cloned.1.call-start = ((), (), s32[]{:S(2)}) async-start(), calls=%async_computation.5 | async-start | bytes 17825792 | tf_op jit(solution)/shard_map/all_gather | solution.py:36
  590.1 116.4 %copy-start.4 = (f32[4,256,256]{2,1,0:T(8,128)S(1)}, f32[4,256,256]{2,1,0:T(8,128)}, u32[]{:S(2)}) copy-start(f32[4,256,256]{2,1,0:T(8,128)} %all-reduce.12.cloned.1.call-done) | copy-start | bytes 3145732
  716.1 7.2 copy-start.1
Sparse Core Ops, SparseCore 0:
  29.6 86.9 all-reduce.5
  182.6 59.5 all-reduce.7
  244.6 110.7 all-gather.2
  377.1 84.0 all-reduce.9
  525.6 61.5 all-reduce.11
  589.2 110.7 all-gather.4
where the time goes:
time: 800 us; the launch traced here: 791 us
  waiting for transfers between devices  512 us (64%)
  other arithmetic  118 us (15%)
  local copies, waits for them, and re-layouts  71.5 us (9%)
  blocking collectives  39.5 us (5%)
  matrix products  31 us (4%)
  between operations  17.6 us (2%)
    psum x4, waiting for transfers between devices, from_root(): return lax.psum(kept, axis)  289 us
    all_gather x2, waiting for transfers between devices, shards(): whole = lax.all_gather(solved, 'row', axis=0, tiled=True)  223 us
    another operation x13, other arithmetic, shards(): factor = jnp.linalg.cholesky(corner)  68.7 us
    unnamed x12, local copies, waits for them, and re-layouts  44.5 us
    psum x1, blocking collectives, shards(): checksum = lax.psum(partial_sums, 'row')  39.5 us
    another operation x5, other arithmetic, shards(): solved = jax.scipy.linalg.solve_triangular(factor, column.T, lower=True).T  39.4 us
    dot_general x2, matrix products, shards(): jnp.einsum('iak,jbk->iajb', solved, across, precision=HIGHEST)  19.2 us
  transfers between devices with their start and end apart: 6, of which 6 were waited for; matrix products, arithmetic and copies ran while one was open for 1% of the time, Pallas kernels for 0%

commit v1 on v0

--- a/solution.py
+++ b/solution.py
@@ -42,7 +42,7 @@
     trailing = jnp.where(keep, matrix, 0.0)
     weights = check_weights.reshape(row_tiles, width)
     partial_sums = jnp.einsum("ia,iajb->jb", weights, trailing, precision=HIGHEST)
-    checksum = lax.psum(partial_sums, "row")
+    checksum = jnp.sum(lax.all_gather(partial_sums, "row"), axis=0)
     panels = jnp.concatenate(panel_list, axis=2)
     return (
         trailing.reshape(row_tiles, 1, width, col_tiles, 1, width),

time: 800 us -> 785 us (0.981)
  blocking collectives: 39.5 us -> 23.3 us
    psum x1 -> x0, blocking collectives: 39.5 us -> none  [shards(): checksum = lax.psum(partial_sums, 'row')]
    all_gather x0 -> x1, blocking collectives: none -> 23.3 us  [shards(): checksum = jnp.sum(lax.all_gather(partial_sums, 'row'), axis=0)]
    unnamed x12 -> x13, local copies, waits for them, and re-layouts: 44.5 us -> 45.1 us
where the time goes in v1:
time: 785 us; the launch traced here: 775 us
  waiting for transfers between devices  512 us (65%)
  other arithmetic  118 us (15%)
  local copies, waits for them, and re-layouts  72.1 us (9%)
  matrix products  31 us (4%)
  blocking collectives  23.3 us (3%)
  between operations  17.6 us (2%)
    psum x4, waiting for transfers between devices, from_root(): return lax.psum(kept, axis)  289 us
    all_gather x2, waiting for transfers between devices, shards(): whole = lax.all_gather(solved, 'row', axis=0, tiled=True)  223 us
    another operation x13, other arithmetic, shards(): factor = jnp.linalg.cholesky(corner)  68.7 us
    unnamed x13, local copies, waits for them, and re-layouts  45.1 us
    another operation x5, other arithmetic, shards(): solved = jax.scipy.linalg.solve_triangular(factor, column.T, lower=True).T  39.4 us
    all_gather x1, blocking collectives, shards(): checksum = jnp.sum(lax.all_gather(partial_sums, 'row'), axis=0)  23.3 us
    dot_general x2, matrix products, shards(): jnp.einsum('iak,jbk->iajb', solved, across, precision=HIGHEST)  19.2 us
  transfers between devices with their start and end apart: 6, of which 6 were waited for; matrix products, arithmetic and copies ran while one was open for 1% of the time, Pallas kernels for 0%

profile of v1, /device:TPU:0, one launch (start us, length us, event | category | flops | bytes accessed | tf_op | source)
XLA Modules:
  0.0 775.0 jit_solution(17359477412952875193)
XLA Ops:
  7.2 20.6 %copy.38 = f32[4,1,256,8,1,256]{2,5,3,0,4,1:T(8,128)} copy(f32[4,1,256,8,1,256]{5,4,3,2,1,0:T(1,128)} %param.7) | data formatting | bytes 16777216 | tf_op args[0]
  27.8 1.7 fusion.15
  29.5 1.3 slice.67
  31.5 85.0 %all-reduce.6.cloned.1.call-done = f32[256,256]{0,1:T(8,128)} async-done(((f32[256,256]{0,1:T(8,128)}), f32[256,256]{0,1:T(8,128)}) %all-reduce.6.cloned.1.call-update) | async-done | bytes 262160 | tf_op jit(solution)/shard_map/psum | solution.py:11
  116.6 1.0 convert_select_fusion.1
  117.7 1.0 fusion.17
  118.7 11.7 %cholesky.130 = f32[128,128]{1,0:T(8,128)S(1)} custom-call(f32[128,128]{1,0:T(8,128)S(1)} %cholesky.194), custom_call_target="Cholesky" | custom-call | tf_op jit(solution)/shard_map/jit(cholesky)/cholesky | solution.py:30
  130.4 9.8 %custom-call.13 = f32[1,128,128]{1,2,0:T(8,128)S(1)} custom-call(f32[1,128,128]{2,1,0:T(8,128)S(1)} %get-tuple-element.61), custom_call_target="InvertDiagBlocksLowerTriangular" | custom-call | tf_op jit(solution)/shard_map/jit(cholesky)/cholesky | solution.py:30
  140.8 11.7 %cholesky.147 = f32[128,128]{1,0:T(8,128)S(1)} custom-call(f32[128,128]{1,0:T(8,128)S(1)} %convolution_subtract_fusion.4), custom_call_target="Cholesky" | custom-call | tf_op jit(solution)/shard_map/jit(cholesky)/cholesky | solution.py:30
  152.5 0.7 compare_reduce_fusion.2
  154.7 4.6 while.4
  155.2 0.6 fusion.48
  155.8 1.4 bitcast_dynamic-update-slice_fusion.4
  157.3 0.6 fusion.48
  157.9 1.4 bitcast_dynamic-update-slice_fusion.4
  159.3 19.7 %custom-call.14 = f32[2,128,128]{1,2,0:T(8,128)S(1)} custom-call(f32[2,128,128]{2,1,0:T(8,128)S(1)} %get-tuple-element.20), custom_call_target="InvertDiagBlocksLowerTriangular" | custom-call | tf_op jit(solution)/shard_map/jit(_solve_triangular)/triangular_solve | solution.py:32
  179.0 0.6 fusion.12
  180.2 0.6 fusion.23
  181.3 1.2 select_select_fusion.1
  182.5 59.7 %all-reduce.8.cloned.1.call-done = f32[4,256,256]{2,1,0:T(8,128)} async-done(((f32[4,256,256]{2,1,0:T(8,128)}), f32[4,256,256]{2,1,0:T(8,128)}) %all-reduce.8.cloned.1.call-update) | async-done | bytes 1048592 | tf_op jit(solution)/shard_map/psum | solution.py:11
  242.4 113.1 %all-gather.4.cloned.1.call-done = f32[64,256,256]{2,1,0:T(8,128)} async-done(((f32[4,256,256]{2,1,0:T(8,128)}), f32[64,256,256]{2,1,0:T(8,128)}) %all-gather.4.cloned.1.call-update) | async-done | bytes 16777232 | tf_op jit(solution)/shard_map/all_gather | solution.py:36
  355.4 7.8 %gather_fusion = f32[8,256,256]{2,1,0:T(8,128)} fusion(f32[64,256,256]{2,1,0:T(8,128)} %all-gather.4.cloned.1.call-done, s32[1024]{0:T(1024)S(1)} %pad_clamp_fusion), kind=kCustom, calls=%fused_computation.clone | custom fusion | bytes 4194336 | tf_op jit(solution)/shard_map/jit(_take)/gather | solution.py:38
  363.2 9.6 %convolution_subtract_fusion = f32[4,256,8,256]{1,3,2,0:T(8,128)S(1)} fusion(f32[8,256,256]{2,1,0:T(8,128)} %gather_fusion, f32[4,256,256]{2,1,0:T(8,128)S(1)} %copy-done.3, pred[8]{0:T(512)(128)(4,1)S(1)} %compare_and_fusion, f32[4,1,256,8,1,256]{2,5,3,0,4,1:T(8,128)} %copy.38), kind=kOutput, calls=%fused_computation.7 | convolution fusion | flops 6445072384 | bytes 19922952 | tf_op jit(solution)/shard_map/iak,jbk->iajb/dot_general | solution.py:39
  372.8 3.4 copy-done.2
  376.2 0.7 fusion.14
  377.2 1.0 slice-done
  378.8 82.3 %all-reduce.10.cloned.1.call-done = f32[256,256]{0,1:T(8,128)} async-done(((f32[256,256]{0,1:T(8,128)}), f32[256,256]{0,1:T(8,128)}) %all-reduce.10.cloned.1.call-update) | async-done | bytes 262160 | tf_op jit(solution)/shard_map/psum | solution.py:11
  461.4 11.7 %cholesky.164 = f32[128,128]{1,0:T(8,128)S(1)} custom-call(f32[128,128]{1,0:T(8,128)S(1)} %cholesky.197), custom_call_target="Cholesky" | custom-call | tf_op jit(solution)/shard_map/jit(cholesky)/cholesky | solution.py:30
  473.1 0.6 compare_reduce_fusion.1
  473.8 9.8 %custom-call.15 = f32[1,128,128]{1,2,0:T(8,128)S(1)} custom-call(f32[1,128,128]{2,1,0:T(8,128)S(1)} %get-tuple-element.57), custom_call_target="InvertDiagBlocksLowerTriangular" | custom-call | tf_op jit(solution)/shard_map/jit(cholesky)/cholesky | solution.py:30
  484.1 11.7 %cholesky.181 = f32[128,128]{1,0:T(8,128)S(1)} custom-call(f32[128,128]{1,0:T(8,128)S(1)} %convolution_subtract_fusion.3), custom_call_target="Cholesky" | custom-call | tf_op jit(solution)/shard_map/jit(cholesky)/cholesky | solution.py:30
  495.9 0.7 compare_reduce_fusion
  498.0 4.3 while.5
  498.8 1.4 bitcast_dynamic-update-slice_fusion.5
  500.9 1.4 bitcast_dynamic-update-slice_fusion.5
  502.3 19.7 %custom-call.16 = f32[2,128,128]{1,2,0:T(8,128)S(1)} custom-call(f32[2,128,128]{2,1,0:T(8,128)S(1)} %get-tuple-element.21), custom_call_target="InvertDiagBlocksLowerTriangular" | custom-call | tf_op jit(solution)/shard_map/jit(_solve_triangular)/triangular_solve | solution.py:32
  522.0 0.6 fusion.10
  523.2 0.6 fusion.19
  524.3 1.2 select_select_fusion
  525.5 61.7 %all-reduce.12.cloned.1.call-done = f32[4,256,256]{2,1,0:T(8,128)} async-done(((f32[4,256,256]{2,1,0:T(8,128)}), f32[4,256,256]{2,1,0:T(8,128)}) %all-reduce.12.cloned.1.call-update) | async-done | bytes 1048592 | tf_op jit(solution)/shard_map/psum | solution.py:11
  587.3 2.8 maximum_bitcast_fusion
  590.1 109.9 %all-gather.6.cloned.1.call-done = f32[64,256,256]{2,1,0:T(8,128)} async-done(((f32[4,256,256]{2,1,0:T(8,128)}), f32[64,256,256]{2,1,0:T(8,128)}) %all-gather.6.cloned.1.call-update) | async-done | bytes 16777232 | tf_op jit(solution)/shard_map/all_gather | solution.py:36
  700.0 6.4 gather_fusion.1
  706.5 9.6 %subtract_select_fusion = f32[4,256,8,256]{1,3,2,0:T(8,128)S(1)} fusion(f32[4,256,8,256]{1,3,2,0:T(8,128)} %copy-done.2, pred[4,8]{1,0:T(4,128)(4,1)S(1)} %broadcast_and_fusion, f32[8,256,256]{2,1,0:T(8,128)S(1)} %gather_fusion.1, f32[4,256,256]{2,1,0:T(8,128)S(1)} %copy-done.4, pred[8]{0:T(512)(128)(4,1)S(1)} %compare_and_fusion), kind=kOutput, calls=%fused_computation.6 | convolution fusion | flops 6447169536 | bytes 19922984 | tf_op jit(solution)/shard_map/iak,jbk->iajb/dot_general | solution.py:39
  716.1 7.2 fusion.28
  723.3 23.3 %all-gather = f32[128,256]{1,0:T(8,128)S(1)} all-gather(f32[8,256]{1,0:T(8,128)S(1)} %bitcast.120), channel_id=2, replica_groups=mesh['row'=16,'col'=8] {'row'}, dimensions={0}, use_global_device_ids=true | all-gather | bytes 139264 | tf_op jit(solution)/shard_map/all_gather | solution.py:45
  746.6 0.6 copy.51
  747.2 20.5 %copy.49 = f32[4,1,256,8,1,256]{5,4,3,2,1,0:T(1,128)} copy(f32[4,1,256,8,1,256]{2,5,3,0,4,1:T(8,128)} %bitcast.109) | data formatting | bytes 16777216
  (70 shorter events, 6.9 us)
Async XLA Ops:
  7.2 708.9 %copy-start = (f32[4,1,256]{2,1,0:T(1,128)S(1)}, f32[4,1,256]{2,1,0:T(1,128)}, u32[]{:S(2)}) copy-start(f32[4,1,256]{2,1,0:T(1,128)} %param.8) | copy-start | bytes 12292
  7.2 109.4 %all-reduce.6.cloned.1.call-start = ((), (), s32[]{:S(2)}) async-start(), calls=%async_computation | async-start | bytes 524288 | tf_op jit(solution)/shard_map/psum | solution.py:11
  29.5 212.7 %all-reduce.8.cloned.1.call-start = ((), (), s32[]{:S(2)}) async-start(), calls=%async_computation.1 | async-start | bytes 2097152 | tf_op jit(solution)/shard_map/psum | solution.py:11
  182.5 173.0 %all-gather.4.cloned.1.call-start = ((), (), s32[]{:S(2)}) async-start(), calls=%async_computation.2 | async-start | bytes 17825792 | tf_op jit(solution)/shard_map/all_gather | solution.py:36
  242.2 218.9 %all-reduce.10.cloned.1.call-start = ((), (), s32[]{:S(2)}) async-start(), calls=%async_computation.3 | async-start | bytes 524288 | tf_op jit(solution)/shard_map/psum | solution.py:11
  242.4 120.8 %copy-start.3 = (f32[4,256,256]{2,1,0:T(8,128)S(1)}, f32[4,256,256]{2,1,0:T(8,128)}, u32[]{:S(2)}) copy-start(f32[4,256,256]{2,1,0:T(8,128)} %all-reduce.8.cloned.1.call-done) | copy-start | bytes 3145732
  372.8 3.4 copy-start.2
  376.9 1.2 slice-start
  377.0 210.2 %all-reduce.12.cloned.1.call-start = ((), (), s32[]{:S(2)}) async-start(), calls=%async_computation.4 | async-start | bytes 2097152 | tf_op jit(solution)/shard_map/psum | solution.py:11
  525.5 174.6 %all-gather.6.cloned.1.call-start = ((), (), s32[]{:S(2)}) async-start(), calls=%async_computation.5 | async-start | bytes 17825792 | tf_op jit(solution)/shard_map/all_gather | solution.py:36
  590.1 116.4 %copy-start.4 = (f32[4,256,256]{2,1,0:T(8,128)S(1)}, f32[4,256,256]{2,1,0:T(8,128)}, u32[]{:S(2)}) copy-start(f32[4,256,256]{2,1,0:T(8,128)} %all-reduce.12.cloned.1.call-done) | copy-start | bytes 3145732
  716.1 7.2 copy-start.1
Sparse Core Ops, SparseCore 0:
  29.6 86.9 all-reduce.5
  182.6 59.5 all-reduce.7
  244.6 110.7 all-gather.3
  377.1 84.0 all-reduce.9
  525.6 61.5 all-reduce.11
  589.2 110.7 all-gather.5
